TPU v7x, 128 devices: a whole 4x4x4 slice. The times are simulated.
128 devices in a mesh: row: 8 (over x, z_lo), col: 16 (over y, z_hi, core).
Axes of the slice: x: 4, y: 4, z: 4 (z_hi: 2, z_lo: 2; z = z_hi * 2 + z_lo), core: 2. Of those that a mesh axis runs over, the one named last changes fastest.
Arguments:
- tokens_in: bfloat16 [8192, 5120], P('row', 'col'), may hold values from -6 to 6
- token_grad: bfloat16 [8192, 5120], P('row', 'col'), may hold values from -6 to 6
- gate_gain: float32 [5120], replicated, may hold values from -4 to 4
- inner_weight: bfloat16 [5120, 13824], P(None, 'col'), may hold values from -0.078125 to 0.078125
- inner_bias: float32 [13824], P('col'), may hold values from -4 to 4
- outer_weight: bfloat16 [5120, 13824], P(None, 'col'), may hold values from -0.0546875 to 0.0546875
- inner_down: bfloat16 [5120, 64], replicated, may hold values from -0.078125 to 0.078125
- inner_up: bfloat16 [64, 13824], P(None, 'col'), may hold values from -0.1796875 to 0.1796875
- outer_down: bfloat16 [13824, 64], P('col'), may hold values from -0.0546875 to 0.0546875
- outer_up: bfloat16 [64, 5120], replicated, may hold values from -0.1796875 to 0.1796875
Outputs:
- tokens_grad: bfloat16 [8192, 5120], P('row', 'col')
- inner_down_grad: float32 [5120, 64], P('col')
- inner_up_grad: float32 [64, 13824], P(None, 'col')
- outer_down_grad: float32 [13824, 64], P('col')
- outer_up_grad: float32 [64, 5120], P(None, 'col')
All inputs are finite; a program needn't handle non-finite values.
Results may differ from a plain program's by a relative error of at most 0.023.
Values may be sent and summed in bfloat16 or wider, within the bound.
A program may use at most 128 MiB of HBM per device.

v0:
```python
import math
import jax
import jax.numpy as jnp
from jax import lax
from jax.sharding import Mesh
from jax.sharding import PartitionSpec as P

SLOPE_SCALE = 0.7978845608028654
CUBIC = 0.044715
COL = ("cc", "core")


def gelu_value(pre):
    inner = SLOPE_SCALE * (pre + CUBIC * pre * pre * pre)
    return 0.5 * pre * (1.0 + jnp.tanh(inner))


def gelu_slope(pre):
    tangent = jnp.tanh(SLOPE_SCALE * (pre + CUBIC * pre * pre * pre))
    return 0.5 * (1.0 + tangent) + 0.5 * pre * (1.0 - tangent * tangent) * SLOPE_SCALE * (
        1.0 + 3.0 * CUBIC * pre * pre
    )


def plain_dot(left, right):
    return jnp.dot(left, right, preferred_element_type=jnp.float32)


def dot_rows(left, right):
    return lax.dot_general(
        left, right, (((1,), (1,)), ((), ())), preferred_element_type=jnp.float32
    )


def dot_cols(left, right):
    return lax.dot_general(
        left, right, (((0,), (0,)), ((), ())), preferred_element_type=jnp.float32
    )


def tree_sum(value, axis, size):
    step = 1
    while step < size:
        pairs = [(i, i ^ step) for i in range(size)]
        value = value + lax.ppermute(value, axis, pairs)
        step *= 2
    return value


def core_major(rows, n_cc, n_core):
    shape = rows.shape
    split = rows.reshape((n_cc, n_core, shape[0] // (n_cc * n_core)) + shape[1:])
    return jnp.swapaxes(split, 0, 1).reshape(shape)


def gather_features(block, n_cc, n_core):
    over_chips = lax.all_gather(block, "cc", axis=1, tiled=True)
    return lax.all_gather(over_chips, "core", axis=1, tiled=True)


def local(
    tokens_in,
    token_grad,
    gate_gain,
    inner_weight,
    inner_bias,
    outer_weight,
    inner_down,
    inner_up,
    outer_down,
    outer_up,
):
    n_cc = lax.axis_size("cc")
    n_core = lax.axis_size("core")
    n_col = n_cc * n_core
    n_row = lax.axis_size("row")
    col_index = lax.axis_index("cc") * n_core + lax.axis_index("core")
    local_width = token_grad.shape[1]
    tok_rows = tokens_in.shape[0]
    ff_local = inner_weight.shape[1]
    rank = inner_down.shape[1]
    gain_local = lax.dynamic_slice_in_dim(gate_gain, col_index * local_width, local_width, 0)
    gated_local = (gain_local[None, :] * token_grad.astype(jnp.float32)).astype(jnp.bfloat16)
    tokens_full = gather_features(tokens_in, n_cc, n_core)
    gated_full = gather_features(gated_local, n_cc, n_core)
    inner_weight_p = core_major(inner_weight, n_cc, n_core)
    outer_weight_p = core_major(outer_weight, n_cc, n_core)
    inner_down_p = core_major(inner_down, n_cc, n_core)
    outer_up_p = core_major(outer_up.T, n_cc, n_core)
    inner_low = plain_dot(tokens_full, inner_down_p).astype(jnp.bfloat16)
    forward_sum = plain_dot(tokens_full, inner_weight_p)
    grad_low = plain_dot(gated_full, outer_up_p).astype(jnp.bfloat16)
    backward_sum = plain_dot(gated_full, outer_weight_p)
    pre = forward_sum + plain_dot(inner_low, inner_up) + inner_bias[None, :]
    hidden = gelu_value(pre).astype(jnp.bfloat16)
    grad_hidden = backward_sum + dot_rows(grad_low, outer_down)
    grad_pre = (grad_hidden * gelu_slope(pre)).astype(jnp.bfloat16)
    pre_low_part = dot_rows(grad_pre, inner_up)
    block_part = dot_rows(grad_pre, inner_weight_p).astype(jnp.bfloat16).astype(jnp.float32)
    low_part = dot_rows(pre_low_part.astype(jnp.bfloat16), inner_down_p)
    summed = (block_part + low_part).astype(jnp.bfloat16)
    on_chip = lax.psum_scatter(summed, "core", scatter_dimension=1, tiled=True)
    tokens_grad = lax.psum_scatter(on_chip, "cc", scatter_dimension=1, tiled=True)
    hidden_low_part = plain_dot(hidden, outer_down)
    lows = tree_sum(jnp.concatenate([hidden_low_part, pre_low_part], axis=1), COL, n_col)
    hidden_low = lows[:, :rank].astype(jnp.bfloat16)
    pre_low = lows[:, rank:].astype(jnp.bfloat16)
    scale = 1.0 / math.sqrt(tok_rows * n_row)
    outer_down_term = dot_cols(hidden, grad_low)
    outer_up_term = dot_cols(gated_local, hidden_low)
    inner_down_term = dot_cols(tokens_in, pre_low)
    inner_up_term = dot_cols(grad_pre, inner_low)
    packed = jnp.concatenate(
        [outer_down_term, inner_up_term, outer_up_term, inner_down_term], axis=0
    )
    packed = tree_sum(packed, "row", n_row) * scale
    outer_down_grad = packed[:ff_local]
    inner_up_grad = packed[ff_local : 2 * ff_local].T
    outer_up_grad = packed[2 * ff_local : 2 * ff_local + local_width].T
    inner_down_grad = packed[2 * ff_local + local_width :]
    return (tokens_grad, inner_down_grad, inner_up_grad, outer_down_grad, outer_up_grad)


def solution(mesh):
    n_row, n_col = mesh.devices.shape
    split = Mesh(mesh.devices.reshape(n_row, n_col // 2, 2), ("row", "cc", "core"))
    placed = (
        P("row", COL),
        P("row", COL),
        P(),
        P(None, COL),
        P(COL),
        P(None, COL),
        P(),
        P(None, COL),
        P(COL, None),
        P(),
    )
    return jax.shard_map(
        local,
        mesh=split,
        in_specs=placed,
        out_specs=(P("row", COL), P(COL, None), P(None, COL), P(COL, None), P(None, COL)),
        check_vma=False,
    )
```

profile of v0, /device:TPU:8, one launch (start us, length us, event | category | flops | bytes accessed | tf_op | source)
XLA Modules:
  0.0 452.8 jit_solution(1446664084841437667)
XLA Ops:
  7.2 0.0 all-gather.5.cloned.1.call-start
  7.2 0.8 dynamic_slice.3
  8.0 2.1 multiply_convert_fusion.1
  10.1 0.0 all-gather.9.cloned.1.call-start
  10.2 0.7 all-gather.9.cloned.1.call-update
  10.9 0.0 all-gather.7.cloned.1.call-start
  10.9 80.9 %all-gather.5.cloned.1.call-done = bf16[1024,2560]{0,1:T(8,128)(2,1)} async-done(((bf16[1024,320]{0,1:T(8,128)(2,1)}), bf16[1024,2560]{0,1:T(8,128)(2,1)}) %all-gather.5.cloned.1.call-update) | async-done | bytes 5242896 | tf_op jit(solution)/shard_map/all_gather | solution.py:57
  91.8 0.0 all-gather.11.cloned.1.call-start
  91.9 80.3 %all-gather.9.cloned.1.call-done = bf16[1024,2560]{0,1:T(8,128)(2,1)} async-done(((bf16[1024,320]{0,1:T(8,128)(2,1)}), bf16[1024,2560]{0,1:T(8,128)(2,1)}) %all-gather.9.cloned.1.call-update) | async-done | bytes 5242896 | tf_op jit(solution)/shard_map/all_gather | solution.py:57
  172.2 0.0 reduce-scatter.5.cloned.1.call-start
  172.3 0.8 reshape.42
  173.1 0.1 copy.34
  173.3 0.6 reshape.43
  173.9 0.8 reshape.38
  174.8 0.1 copy.35
  174.9 0.6 reshape.39
  175.5 13.5 %copy.26 = bf16[5120,864]{1,0:T(8,128)(2,1)} copy(bf16[5120,864]{0,1:T(8,128)(2,1)} %param.13) | data formatting | bytes 17694720 | tf_op args[3]
  189.0 9.7 %copy.27 = bf16[2,8,320,864]{3,2,1,0:T(8,128)(2,1)} copy(bf16[2,8,320,864]{3,2,0,1:T(8,128)(2,1)} %bitcast.60) | data formatting | bytes 17694720 | tf_op jit(solution)/shard_map/transpose | solution.py:53
  198.7 12.9 %copy.23 = bf16[5120,864]{1,0:T(8,128)(2,1)} copy(bf16[5120,864]{0,1:T(8,128)(2,1)} %param.15) | data formatting | bytes 17694720 | tf_op args[5]
  211.6 11.2 %copy.24 = bf16[2,8,320,864]{3,2,1,0:T(8,128)(2,1)} copy(bf16[2,8,320,864]{3,2,0,1:T(8,128)(2,1)} %bitcast.61) | data formatting | bytes 17694720 | tf_op jit(solution)/shard_map/transpose | solution.py:53
  222.7 5.9 %convolution_convert_fusion.1 = bf16[1024,64]{0,1:T(8,128)(2,1)S(1)} fusion(bf16[5120,64]{0,1:T(8,128)(2,1)S(1)} %reshape.39, bf16[1024,5120]{0,1:T(8,128)(2,1)} %all-gather.7.cloned.1.call-done), kind=kOutput, calls=%fused_computation.14 | convolution fusion | flops 671154176 | bytes 11272192 | tf_op jit(solution)/shard_map/dot_general | solution.py:26
  228.7 2.4 fusion.13
  231.2 5.9 %convolution_convert_fusion = bf16[1024,64]{0,1:T(8,128)(2,1)S(1)} fusion(bf16[5120,64]{0,1:T(8,128)(2,1)S(1)} %reshape.43, bf16[1024,5120]{0,1:T(8,128)(2,1)} %all-gather.11.cloned.1.call-done), kind=kOutput, calls=%fused_computation.13 | convolution fusion | flops 671154176 | bytes 11272192 | tf_op jit(solution)/shard_map/dot_general | solution.py:26
  237.1 0.7 fusion.14
  237.8 0.0 copy-done.14
  237.8 17.1 %multiply_convert_fusion = (bf16[1024,864]{0,1:T(8,128)(2,1)S(1)}, f32[1024,864]{0,1:T(8,128)}) fusion(f32[864]{0:T(1024)S(1)} %copy-done.14, f32[1024,864]{0,1:T(8,128)S(1)} %fusion.14, bf16[1024,5120]{0,1:T(8,128)(2,1)} %all-gather.11.cloned.1.call-done, bf16[5120,864]{1,0:T(8,128)(2,1)} %bitcast.63), kind=kOutput, calls=%fused_computation.10 | convolution fusion | flops 9069428736 | bytes 28183936 | tf_op jit(solution)/shard_map/dot_general | solution.py:26
  254.9 18.2 %fusion.6 = bf16[1024,864]{0,1:T(8,128)(2,1)S(1)} fusion(f32[1024,864]{0,1:T(8,128)} %get-tuple-element.25, f32[1024,864]{0,1:T(8,128)} %fusion.13, bf16[1024,5120]{0,1:T(8,128)(2,1)} %all-gather.7.cloned.1.call-done, bf16[5120,864]{1,0:T(8,128)(2,1)} %bitcast.65), kind=kOutput, calls=%fused_computation.9 | convolution fusion | flops 9077391360 | bytes 28180480 | tf_op jit(solution)/shard_map/dot_general | solution.py:26
  273.1 1.2 copy-done.1
  274.3 1.2 fusion.18
  275.5 14.2 %fusion.15 = bf16[1024,5120]{1,0:T(8,128)(2,1)S(1)} fusion(bf16[1024,864]{0,1:T(8,128)(2,1)} %copy-done.1, bf16[5120,864]{1,0:T(8,128)(2,1)} %bitcast.64), kind=kOutput, calls=%fused_computation.31 | convolution fusion | flops 9059696640 | bytes 21102592 | tf_op jit(solution)/shard_map/dot_general | solution.py:30
  289.7 6.7 %add_convert_fusion = bf16[1024,5120]{1,0:T(8,128)(2,1)} fusion(bf16[5120,64]{0,1:T(8,128)(2,1)S(1)} %reshape.43, bf16[1024,5120]{1,0:T(8,128)(2,1)S(1)} %fusion.15, f32[1024,64]{0,1:T(8,128)} %fusion.18), kind=kOutput, calls=%fused_computation | convolution fusion | flops 686882816 | bytes 21889024 | tf_op jit(solution)/shard_map/dot_general | solution.py:30
  296.5 0.0 reduce-scatter.7.cloned.1.call-start
  296.5 20.7 %reduce-scatter.5.cloned.1.call-done = bf16[1024,2560]{1,0:T(8,128)(2,1)} async-done(((bf16[1024,5120]{1,0:T(8,128)(2,1)}), bf16[1024,2560]{1,0:T(8,128)(2,1)}) %reduce-scatter.5.cloned.1.call-update) | async-done | bytes 5242896 | tf_op jit(solution)/shard_map/reduce_scatter | solution.py:102
  317.2 8.0 %copy.30 = bf16[1024,2560]{0,1:T(8,128)(2,1)} copy(bf16[1024,2560]{1,0:T(8,128)(2,1)} %reduce-scatter.5.cloned.1.call-done) | data formatting | bytes 10485760
  325.2 0.9 copy-done.13
  326.1 0.4 fusion.19
  326.6 0.3 collective-permute-start
  326.9 1.7 collective-permute-done
  328.6 0.1 fusion.11
  328.6 3.2 collective-permute-start.1
  331.9 18.6 %collective-permute-done.1 = f32[1024,128]{0,1:T(8,128)S(1)} collective-permute-done((f32[1024,128]{0,1:T(8,128)S(1)}, f32[1024,128]{0,1:T(8,128)S(1)}, u32[]{:S(2)}, u32[]{:S(2)}) %collective-permute-start.1) | collective-permute-done | bytes 524320 | tf_op jit(solution)/shard_map/ppermute | solution.py:45
  350.5 0.1 add.74
  350.5 0.6 collective-permute-start.2
  351.2 24.2 %collective-permute-done.2 = f32[1024,128]{0,1:T(8,128)S(1)} collective-permute-done((f32[1024,128]{0,1:T(8,128)S(1)}, f32[1024,128]{0,1:T(8,128)S(1)}, u32[]{:S(2)}, u32[]{:S(2)}) %collective-permute-start.2) | collective-permute-done | bytes 524320 | tf_op jit(solution)/shard_map/ppermute | solution.py:45
  375.4 0.1 add.75
  375.5 2.5 collective-permute-start.3
  377.9 0.6 fusion.16
  378.6 0.6 fusion.17
  379.3 12.0 %collective-permute-done.3 = f32[1024,128]{0,1:T(8,128)S(1)} collective-permute-done((f32[1024,128]{0,1:T(8,128)S(1)}, f32[1024,128]{0,1:T(8,128)S(1)}, u32[]{:S(2)}, u32[]{:S(2)}) %collective-permute-start.3) | collective-permute-done | bytes 524320 | tf_op jit(solution)/shard_map/ppermute | solution.py:45
  391.3 0.1 add_convert_fusion.1
  391.3 0.3 fusion.8
  391.7 0.3 convolution_bitcast_fusion
  392.0 0.2 concatenate.7
  392.2 1.1 collective-permute-start.4
  393.3 19.4 %collective-permute-done.4 = f32[2368,64]{0,1:T(8,128)S(1)} collective-permute-done((f32[2368,64]{0,1:T(8,128)S(1)}, f32[2368,64]{0,1:T(8,128)S(1)}, u32[]{:S(2)}, u32[]{:S(2)}) %collective-permute-start.4) | collective-permute-done | bytes 606240 | tf_op jit(solution)/shard_map/ppermute | solution.py:45
  412.7 0.1 add.77
  412.8 1.5 collective-permute-start.5
  414.2 14.0 %collective-permute-done.5 = f32[2368,64]{0,1:T(8,128)S(1)} collective-permute-done((f32[2368,64]{0,1:T(8,128)S(1)}, f32[2368,64]{0,1:T(8,128)S(1)}, u32[]{:S(2)}, u32[]{:S(2)}) %collective-permute-start.5) | collective-permute-done | bytes 606240 | tf_op jit(solution)/shard_map/ppermute | solution.py:45
  428.2 0.1 add.78
  428.2 3.0 collective-permute-start.6
  431.3 13.0 %collective-permute-done.6 = f32[2368,64]{0,1:T(8,128)S(1)} collective-permute-done((f32[2368,64]{0,1:T(8,128)S(1)}, f32[2368,64]{0,1:T(8,128)S(1)}, u32[]{:S(2)}, u32[]{:S(2)}) %collective-permute-start.6) | collective-permute-done | bytes 606240 | tf_op jit(solution)/shard_map/ppermute | solution.py:45
  444.3 0.1 add_multiply_fusion
  444.4 0.7 slice_bitcast_fusion.1
  445.2 0.8 fusion.12
  (36 shorter events, 0.2 us)
Async XLA Ops:
  7.2 229.9 %copy-start = (bf16[64,864]{1,0:T(8,128)(2,1)S(1)}, bf16[64,864]{1,0:T(8,128)(2,1)}, u32[]{:S(2)}) copy-start(bf16[64,864]{1,0:T(8,128)(2,1)} %param.17) | copy-start | bytes 331780
  7.2 84.6 %all-gather.5.cloned.1.call-start = ((), (), s32[]{:S(2)}) async-start(), calls=%async_computation.2 | async-start | bytes 5898240 | tf_op jit(solution)/shard_map/all_gather | solution.py:57
  10.1 162.1 %all-gather.9.cloned.1.call-start = ((), (), s32[]{:S(2)}) async-start(), calls=%async_computation.4 | async-start | bytes 5898240 | tf_op jit(solution)/shard_map/all_gather | solution.py:57
  10.9 211.9 %all-gather.7.cloned.1.call-start = ((), (), s32[]{:S(2)}) async-start(), calls=%async_computation.3 | async-start | bytes 15728640 | tf_op jit(solution)/shard_map/all_gather | solution.py:58
  91.8 80.5 %copy-start.10 = (bf16[5120,64]{0,1:T(8,128)(2,1)S(1)}, bf16[5120,64]{0,1:T(8,128)(2,1)}, u32[]{:S(2)}) copy-start(bf16[5120,64]{0,1:T(8,128)(2,1)} %param.16) | copy-start | bytes 1966084
  91.8 139.3 %all-gather.11.cloned.1.call-start = ((), (), s32[]{:S(2)}) async-start(), calls=%async_computation.5 | async-start | bytes 15728640 | tf_op jit(solution)/shard_map/all_gather | solution.py:58
  172.2 1.7 copy-start.11
  172.2 145.0 %reduce-scatter.5.cloned.1.call-start = ((), (), s32[]{:S(2)}) async-start(), calls=%async_computation.6 | async-start | bytes 15728640 | tf_op jit(solution)/shard_map/reduce_scatter | solution.py:102
  222.7 6.0 %copy-start.12 = (bf16[864,64]{0,1:T(8,128)(2,1)S(1)}, bf16[864,64]{0,1:T(8,128)(2,1)}, u32[]{:S(2)}) copy-start(bf16[864,64]{0,1:T(8,128)(2,1)} %param.18) | copy-start | bytes 331780
  228.7 8.4 %copy-start.6 = (bf16[1024,64]{0,1:T(8,128)(2,1)}, bf16[1024,64]{0,1:T(8,128)(2,1)S(1)}, u32[]{:S(2)}) copy-start(bf16[1024,64]{0,1:T(8,128)(2,1)S(1)} %convolution_convert_fusion.1) | copy-start | bytes 393220
  237.1 17.8 %copy-start.8 = (bf16[1024,64]{0,1:T(8,128)(2,1)}, bf16[1024,64]{0,1:T(8,128)(2,1)S(1)}, u32[]{:S(2)}) copy-start(bf16[1024,64]{0,1:T(8,128)(2,1)S(1)} %convolution_convert_fusion) | copy-start | bytes 393220
  237.1 0.7 copy-start.14
  273.1 1.2 copy-start.1
  296.5 149.5 %reduce-scatter.7.cloned.1.call-start = ((), (), s32[]{:S(2)}) async-start(), calls=%async_computation.7 | async-start | bytes 5898240
  325.2 0.9 copy-start.13
  325.2 1.3 copy-start.3
  326.1 51.9 %copy-start.7 = (bf16[1024,64]{0,1:T(8,128)(2,1)S(1)}, bf16[1024,64]{0,1:T(8,128)(2,1)}, u32[]{:S(2)}) copy-start(bf16[1024,64]{0,1:T(8,128)(2,1)} %copy-done.6) | copy-start | bytes 393220
  326.6 52.0 %copy-start.2 = (bf16[1024,864]{0,1:T(8,128)(2,1)S(1)}, bf16[1024,864]{0,1:T(8,128)(2,1)}, u32[]{:S(2)}) copy-start(bf16[1024,864]{0,1:T(8,128)(2,1)} %copy-done.1) | copy-start | bytes 5308420
  326.6 52.0 %copy-start.9 = (bf16[1024,64]{0,1:T(8,128)(2,1)S(1)}, bf16[1024,64]{0,1:T(8,128)(2,1)}, u32[]{:S(2)}) copy-start(bf16[1024,64]{0,1:T(8,128)(2,1)} %copy-done.8) | copy-start | bytes 393220
  326.6 2.0 collective-permute-start
  328.6 21.8 %collective-permute-start.1 = (f32[1024,128]{0,1:T(8,128)S(1)}, f32[1024,128]{0,1:T(8,128)S(1)}, u32[]{:S(2)}, u32[]{:S(2)}) collective-permute-start(f32[1024,128]{0,1:T(8,128)S(1)} %fusion.11), channel_id=1, source_target_pairs={{0,2},{1,3},{2,0},{3,1},{4,6},{5,7},{6,4},{7,5},{8,10},{9,11},{10,... | collective-permute-start | bytes 1572872 | tf_op jit(solution)/shard_map/ppermute | solution.py:45
  350.5 40.8 %copy-start.4 = (bf16[1024,320]{0,1:T(8,128)(2,1)S(1)}, bf16[1024,320]{0,1:T(8,128)(2,1)}, u32[]{:S(2)}) copy-start(bf16[1024,320]{0,1:T(8,128)(2,1)} %multiply_convert_fusion.1) | copy-start | bytes 1966084
  350.5 24.8 %collective-permute-start.2 = (f32[1024,128]{0,1:T(8,128)S(1)}, f32[1024,128]{0,1:T(8,128)S(1)}, u32[]{:S(2)}, u32[]{:S(2)}) collective-permute-start(f32[1024,128]{0,1:T(8,128)S(1)} %add.74), channel_id=1, source_target_pairs={{0,4},{1,5},{2,6},{3,7},{4,0},{5,1},{6,2},{7,3},{8,12},{9,13},{10,... | collective-permute-start | bytes 1572872 | tf_op jit(solution)/shard_map/ppermute | solution.py:45
  375.5 16.2 %copy-start.5 = (bf16[1024,320]{0,1:T(8,128)(2,1)S(1)}, bf16[1024,320]{0,1:T(8,128)(2,1)}, u32[]{:S(2)}) copy-start(bf16[1024,320]{0,1:T(8,128)(2,1)} %param.10) | copy-start | bytes 1966084
  375.5 15.8 %collective-permute-start.3 = (f32[1024,128]{0,1:T(8,128)S(1)}, f32[1024,128]{0,1:T(8,128)S(1)}, u32[]{:S(2)}, u32[]{:S(2)}) collective-permute-start(f32[1024,128]{0,1:T(8,128)S(1)} %add.75), channel_id=1, source_target_pairs={{0,8},{1,9},{2,10},{3,11},{4,12},{5,13},{6,14},{7,15},{8,0},{9,1},... | collective-permute-start | bytes 1572872 | tf_op jit(solution)/shard_map/ppermute | solution.py:45
  392.2 20.5 %collective-permute-start.4 = (f32[2368,64]{0,1:T(8,128)S(1)}, f32[2368,64]{0,1:T(8,128)S(1)}, u32[]{:S(2)}, u32[]{:S(2)}) collective-permute-start(f32[2368,64]{0,1:T(8,128)S(1)} %concatenate.7), channel_id=1, source_target_pairs={{0,16},{16,0},{32,48},{48,32},{64,80},{80,64},{96,112},{112,96},{1... | collective-permute-start | bytes 1818632 | tf_op jit(solution)/shard_map/ppermute | solution.py:45
  412.8 15.4 %collective-permute-start.5 = (f32[2368,64]{0,1:T(8,128)S(1)}, f32[2368,64]{0,1:T(8,128)S(1)}, u32[]{:S(2)}, u32[]{:S(2)}) collective-permute-start(f32[2368,64]{0,1:T(8,128)S(1)} %add.77), channel_id=1, source_target_pairs={{0,32},{16,48},{32,0},{48,16},{64,96},{80,112},{96,64},{112,80},{1... | collective-permute-start | bytes 1818632 | tf_op jit(solution)/shard_map/ppermute | solution.py:45
  428.2 16.1 %collective-permute-start.6 = (f32[2368,64]{0,1:T(8,128)S(1)}, f32[2368,64]{0,1:T(8,128)S(1)}, u32[]{:S(2)}, u32[]{:S(2)}) collective-permute-start(f32[2368,64]{0,1:T(8,128)S(1)} %add.78), channel_id=1, source_target_pairs={{0,64},{16,80},{32,96},{48,112},{64,0},{80,16},{96,32},{112,48},{1... | collective-permute-start | bytes 1818632 | tf_op jit(solution)/shard_map/ppermute | solution.py:45
Sparse Core Ops, SparseCore 0:
  10.3 81.4 all-gather.4
  94.1 78.0 all-gather.8
  173.9 24.5 all-gather.6
  200.0 26.8 all-gather.10
  296.6 20.5 reduce-scatter.4
  325.3 116.2 reduce-scatter.6
where the time goes:
time: 454 us; the launch traced here: 453 us
  waiting for transfers between devices  286 us (63%)
  matrix products  74.7 us (16%)
  local copies, waits for them, and re-layouts  63.1 us (14%)
  between operations  14.5 us (3%)
  starting transfers between devices  12.4 us (3%)
    all_gather x2, waiting for transfers between devices, gather_features(): over_chips = lax.all_gather(block, 'cc', axis=1, tiled=True)  161 us
    ppermute x7, waiting for transfers between devices, tree_sum(): value = value + lax.ppermute(value, axis, pairs)  103 us
    dot_general x6, matrix products, plain_dot(): return jnp.dot(left, right, preferred_element_type=jnp.float32)  48.2 us
    unnamed x33, local copies, waits for them, and re-layouts  36.5 us
    dot_general x4, matrix products, dot_rows(): lax.dot_general(left, right, (((1,), (1,)), ((), ())), preferred_element_...  24.6 us
    transpose x2, local copies, waits for them, and re-layouts, core_major(): return jnp.swapaxes(split, 0, 1).reshape(shape)  20.9 us
    reduce_scatter x1, waiting for transfers between devices, local(): on_chip = lax.psum_scatter(summed, 'core', scatter_dimension=1, tiled=True)  20.7 us
    ppermute x7, starting transfers between devices, tree_sum(): value = value + lax.ppermute(value, axis, pairs)  12.2 us
  transfers between devices with their start and end apart: 13, of which 10 were waited for; matrix products, arithmetic and copies ran while one was open for 14% of the time, Pallas kernels for 0%

commit v1 on v0

--- a/solution.py
+++ b/solution.py
@@ -54,7 +54,9 @@
 
 
 def gather_features(block, n_cc, n_core):
-    over_chips = lax.all_gather(block, "cc", axis=1, tiled=True)
+    over_chips = jnp.concatenate(
+        lax.all_to_all(jnp.stack([block] * lax.axis_size("cc")), "cc", 0, 0), axis=1
+    )
     return lax.all_gather(over_chips, "core", axis=1, tiled=True)
 
 

time: 454 us -> 424 us (0.934)
  waiting for transfers between devices: 286 us -> 125 us
  blocking collectives: 0 us -> 133 us
    all_gather x2 -> x0, waiting for transfers between devices: 161 us -> none  [gather_features(): over_chips = lax.all_gather(block, 'cc', axis=1, tiled=True)]
    all_to_all x0 -> x2, blocking collectives: none -> 133 us  [gather_features(): lax.all_to_all(jnp.stack([block] * lax.axis_size('cc')), 'cc', 0, 0)]
    unnamed x33 -> x37, local copies, waits for them, and re-layouts: 36.5 us -> 38.5 us
  transfers between devices with their start and end apart: 13 -> 11, of which waited for: 10 -> 8; matrix products, arithmetic and copies ran while one was open for 14% -> 14% of each run, Pallas kernels for 0% -> 0%
where the time goes in v1:
time: 424 us; the launch traced here: 423 us
  blocking collectives  133 us (31%)
  waiting for transfers between devices  125 us (29%)
  matrix products  74.7 us (18%)
  local copies, waits for them, and re-layouts  62 us (15%)
  between operations  14.1 us (3%)
  starting transfers between devices  12.4 us (3%)
    all_to_all x2, blocking collectives, gather_features(): lax.all_to_all(jnp.stack([block] * lax.axis_size('cc')), 'cc', 0, 0)  133 us
    ppermute x7, waiting for transfers between devices, tree_sum(): value = value + lax.ppermute(value, axis, pairs)  103 us
    dot_general x6, matrix products, plain_dot(): return jnp.dot(left, right, preferred_element_type=jnp.float32)  48.1 us
    unnamed x37, local copies, waits for them, and re-layouts  38.5 us
    dot_general x4, matrix products, dot_rows(): lax.dot_general(left, right, (((1,), (1,)), ((), ())), preferred_element_...  24.6 us
    reduce_scatter x1, waiting for transfers between devices, local(): on_chip = lax.psum_scatter(summed, 'core', scatter_dimension=1, tiled=True)  22.1 us
    transpose x2, local copies, waits for them, and re-layouts, core_major(): return jnp.swapaxes(split, 0, 1).reshape(shape)  16.5 us
    ppermute x7, starting transfers between devices, tree_sum(): value = value + lax.ppermute(value, axis, pairs)  12.2 us
  transfers between devices with their start and end apart: 11, of which 8 were waited for; matrix products, arithmetic and copies ran while one was open for 14% of the time, Pallas kernels for 0%

profile of v1, /device:TPU:8, one launch (start us, length us, event | category | flops | bytes accessed | tf_op | source)
XLA Modules:
  0.0 423.1 jit_solution(14367833309599187579)
XLA Ops:
  7.2 0.0 all-gather.3.cloned.1.call-start
  7.2 0.8 dynamic_slice.3
  8.0 1.3 multiply_convert_fusion.1
  9.3 0.7 stack.4
  10.0 68.9 %all_to_all.10 = bf16[8,1024,320]{1,2,0:T(8,128)(2,1)} all-to-all(bf16[8,1024,320]{1,2,0:T(8,128)(2,1)S(1)} %stack.4), channel_id=1, replica_groups=mesh['row'=8,'cc'=8,'core'=2] {'cc'}, dimensions={0} | all-to-all | bytes 10485760 | tf_op jit(solution)/shard_map/all_to_all | solution.py:58
  78.9 0.0 all-gather.5.cloned.1.call-start
  78.9 1.0 copy-done.6
  79.9 0.7 stack.5
  80.6 64.3 %all_to_all.11 = bf16[8,1024,320]{1,2,0:T(8,128)(2,1)} all-to-all(bf16[8,1024,320]{1,2,0:T(8,128)(2,1)S(1)} %stack.5), channel_id=1, replica_groups=mesh['row'=8,'cc'=8,'core'=2] {'cc'}, dimensions={0} | all-to-all | bytes 10485760 | tf_op jit(solution)/shard_map/all_to_all | solution.py:58
  145.0 0.0 reduce-scatter.5.cloned.1.call-start
  145.0 1.0 copy-done.12
  146.0 0.8 reshape.62
  146.9 0.1 copy.36
  147.0 0.6 reshape.63
  147.6 0.8 reshape.56
  148.5 0.1 copy.37
  148.6 0.6 reshape.57
  149.2 13.6 %copy.28 = bf16[5120,864]{1,0:T(8,128)(2,1)} copy(bf16[5120,864]{0,1:T(8,128)(2,1)} %param.13) | data formatting | bytes 17694720 | tf_op args[3]
  162.8 8.6 %copy.29 = bf16[2,8,320,864]{3,2,1,0:T(8,128)(2,1)} copy(bf16[2,8,320,864]{3,2,0,1:T(8,128)(2,1)} %bitcast.66) | data formatting | bytes 17694720 | tf_op jit(solution)/shard_map/transpose | solution.py:53
  171.4 12.8 %copy.25 = bf16[5120,864]{1,0:T(8,128)(2,1)} copy(bf16[5120,864]{0,1:T(8,128)(2,1)} %param.15) | data formatting | bytes 17694720 | tf_op args[5]
  184.2 7.9 %copy.26 = bf16[2,8,320,864]{3,2,1,0:T(8,128)(2,1)} copy(bf16[2,8,320,864]{3,2,0,1:T(8,128)(2,1)} %bitcast.67) | data formatting | bytes 17694720 | tf_op jit(solution)/shard_map/transpose | solution.py:53
  192.1 5.9 %convolution_convert_fusion.1 = bf16[1024,64]{0,1:T(8,128)(2,1)S(1)} fusion(bf16[5120,64]{0,1:T(8,128)(2,1)S(1)} %reshape.57, bf16[1024,5120]{0,1:T(8,128)(2,1)} %all-gather.3.cloned.1.call-done), kind=kOutput, calls=%fused_computation.14 | convolution fusion | flops 671154176 | bytes 11272192 | tf_op jit(solution)/shard_map/dot_general | solution.py:26
  198.1 2.4 fusion.13
  200.5 5.9 %convolution_convert_fusion = bf16[1024,64]{0,1:T(8,128)(2,1)S(1)} fusion(bf16[5120,64]{0,1:T(8,128)(2,1)S(1)} %reshape.63, bf16[1024,5120]{0,1:T(8,128)(2,1)} %all-gather.5.cloned.1.call-done), kind=kOutput, calls=%fused_computation.13 | convolution fusion | flops 671154176 | bytes 11272192 | tf_op jit(solution)/shard_map/dot_general | solution.py:26
  206.5 0.7 fusion.14
  207.2 17.1 %multiply_convert_fusion = (bf16[1024,864]{0,1:T(8,128)(2,1)S(1)}, f32[1024,864]{0,1:T(8,128)}) fusion(f32[864]{0:T(1024)S(1)} %copy-done.16, f32[1024,864]{0,1:T(8,128)S(1)} %fusion.14, bf16[1024,5120]{0,1:T(8,128)(2,1)} %all-gather.5.cloned.1.call-done, bf16[5120,864]{1,0:T(8,128)(2,1)} %bitcast.71), kind=kOutput, calls=%fused_computation.10 | convolution fusion | flops 9069428736 | bytes 28183936 | tf_op jit(solution)/shard_map/dot_general | solution.py:26
  224.2 18.1 %fusion.6 = bf16[1024,864]{0,1:T(8,128)(2,1)S(1)} fusion(f32[1024,864]{0,1:T(8,128)} %get-tuple-element.25, f32[1024,864]{0,1:T(8,128)} %fusion.13, bf16[1024,5120]{0,1:T(8,128)(2,1)} %all-gather.3.cloned.1.call-done, bf16[5120,864]{1,0:T(8,128)(2,1)} %bitcast.73), kind=kOutput, calls=%fused_computation.9 | convolution fusion | flops 9077391360 | bytes 28180480 | tf_op jit(solution)/shard_map/dot_general | solution.py:26
  242.4 1.2 copy-done.1
  243.5 1.2 fusion.18
  244.7 14.2 %fusion.15 = bf16[1024,5120]{1,0:T(8,128)(2,1)S(1)} fusion(bf16[1024,864]{0,1:T(8,128)(2,1)} %copy-done.1, bf16[5120,864]{1,0:T(8,128)(2,1)} %bitcast.72), kind=kOutput, calls=%fused_computation.31 | convolution fusion | flops 9059696640 | bytes 21102592 | tf_op jit(solution)/shard_map/dot_general | solution.py:30
  259.0 6.8 %add_convert_fusion = bf16[1024,5120]{1,0:T(8,128)(2,1)} fusion(bf16[5120,64]{0,1:T(8,128)(2,1)S(1)} %reshape.63, bf16[1024,5120]{1,0:T(8,128)(2,1)S(1)} %fusion.15, f32[1024,64]{0,1:T(8,128)} %fusion.18), kind=kOutput, calls=%fused_computation | convolution fusion | flops 686882816 | bytes 21889024 | tf_op jit(solution)/shard_map/dot_general | solution.py:30
  265.8 0.0 reduce-scatter.7.cloned.1.call-start
  265.8 22.1 %reduce-scatter.5.cloned.1.call-done = bf16[1024,2560]{1,0:T(8,128)(2,1)} async-done(((bf16[1024,5120]{1,0:T(8,128)(2,1)}), bf16[1024,2560]{1,0:T(8,128)(2,1)}) %reduce-scatter.5.cloned.1.call-update) | async-done | bytes 5242896 | tf_op jit(solution)/shard_map/reduce_scatter | solution.py:104
  287.9 8.0 %copy.32 = bf16[1024,2560]{0,1:T(8,128)(2,1)} copy(bf16[1024,2560]{1,0:T(8,128)(2,1)} %reduce-scatter.5.cloned.1.call-done) | data formatting | bytes 10485760
  295.9 0.9 copy-done.15
  296.8 0.4 fusion.19
  297.3 0.3 collective-permute-start
  297.6 1.7 collective-permute-done
  299.3 0.1 fusion.11
  299.3 3.2 collective-permute-start.1
  302.6 18.6 %collective-permute-done.1 = f32[1024,128]{0,1:T(8,128)S(1)} collective-permute-done((f32[1024,128]{0,1:T(8,128)S(1)}, f32[1024,128]{0,1:T(8,128)S(1)}, u32[]{:S(2)}, u32[]{:S(2)}) %collective-permute-start.1) | collective-permute-done | bytes 524320 | tf_op jit(solution)/shard_map/ppermute | solution.py:45
  321.2 0.1 add.74
  321.2 0.6 collective-permute-start.2
  321.8 24.2 %collective-permute-done.2 = f32[1024,128]{0,1:T(8,128)S(1)} collective-permute-done((f32[1024,128]{0,1:T(8,128)S(1)}, f32[1024,128]{0,1:T(8,128)S(1)}, u32[]{:S(2)}, u32[]{:S(2)}) %collective-permute-start.2) | collective-permute-done | bytes 524320 | tf_op jit(solution)/shard_map/ppermute | solution.py:45
  346.1 0.1 add.75
  346.1 2.5 collective-permute-start.3
  348.6 0.6 fusion.16
  349.3 0.7 fusion.17
  349.9 12.0 %collective-permute-done.3 = f32[1024,128]{0,1:T(8,128)S(1)} collective-permute-done((f32[1024,128]{0,1:T(8,128)S(1)}, f32[1024,128]{0,1:T(8,128)S(1)}, u32[]{:S(2)}, u32[]{:S(2)}) %collective-permute-start.3) | collective-permute-done | bytes 524320 | tf_op jit(solution)/shard_map/ppermute | solution.py:45
  361.9 0.1 add_convert_fusion.1
  362.0 0.3 fusion.8
  362.4 0.3 convolution_bitcast_fusion
  362.7 0.2 concatenate.7
  362.9 1.0 collective-permute-start.4
  364.0 19.4 %collective-permute-done.4 = f32[2368,64]{0,1:T(8,128)S(1)} collective-permute-done((f32[2368,64]{0,1:T(8,128)S(1)}, f32[2368,64]{0,1:T(8,128)S(1)}, u32[]{:S(2)}, u32[]{:S(2)}) %collective-permute-start.4) | collective-permute-done | bytes 606240 | tf_op jit(solution)/shard_map/ppermute | solution.py:45
  383.3 0.1 add.77
  383.4 1.6 collective-permute-start.5
  385.0 13.8 %collective-permute-done.5 = f32[2368,64]{0,1:T(8,128)S(1)} collective-permute-done((f32[2368,64]{0,1:T(8,128)S(1)}, f32[2368,64]{0,1:T(8,128)S(1)}, u32[]{:S(2)}, u32[]{:S(2)}) %collective-permute-start.5) | collective-permute-done | bytes 606240 | tf_op jit(solution)/shard_map/ppermute | solution.py:45
  398.8 0.1 add.78
  398.9 2.9 collective-permute-start.6
  401.8 13.2 %collective-permute-done.6 = f32[2368,64]{0,1:T(8,128)S(1)} collective-permute-done((f32[2368,64]{0,1:T(8,128)S(1)}, f32[2368,64]{0,1:T(8,128)S(1)}, u32[]{:S(2)}, u32[]{:S(2)}) %collective-permute-start.6) | collective-permute-done | bytes 606240 | tf_op jit(solution)/shard_map/ppermute | solution.py:45
  414.9 0.1 add_multiply_fusion
  415.0 0.7 slice_bitcast_fusion.1
  415.8 0.8 fusion.12
  (38 shorter events, 0.2 us)
Async XLA Ops:
  7.2 199.3 %copy-start = (bf16[64,864]{1,0:T(8,128)(2,1)S(1)}, bf16[64,864]{1,0:T(8,128)(2,1)}, u32[]{:S(2)}) copy-start(bf16[64,864]{1,0:T(8,128)(2,1)} %param.17) | copy-start | bytes 331780
  7.2 184.9 %all-gather.3.cloned.1.call-start = ((), (), s32[]{:S(2)}) async-start(), calls=%async_computation.4 | async-start | bytes 15728640 | tf_op jit(solution)/shard_map/all_gather | solution.py:60
  9.3 69.6 %copy-start.4 = (bf16[1024,320]{0,1:T(8,128)(2,1)}, bf16[1024,320]{0,1:T(8,128)(2,1)S(1)}, u32[]{:S(2)}) copy-start(bf16[1024,320]{0,1:T(8,128)(2,1)S(1)} %multiply_convert_fusion.1) | copy-start | bytes 1966084
  78.9 1.1 copy-start.6
  78.9 121.6 %all-gather.5.cloned.1.call-start = ((), (), s32[]{:S(2)}) async-start(), calls=%async_computation.5 | async-start | bytes 15728640 | tf_op jit(solution)/shard_map/all_gather | solution.py:60
  144.9 1.1 copy-start.12
  144.9 2.7 copy-start.13
  145.0 142.9 %reduce-scatter.5.cloned.1.call-start = ((), (), s32[]{:S(2)}) async-start(), calls=%async_computation.6 | async-start | bytes 15728640 | tf_op jit(solution)/shard_map/reduce_scatter | solution.py:104
  192.1 6.0 %copy-start.14 = (bf16[864,64]{0,1:T(8,128)(2,1)S(1)}, bf16[864,64]{0,1:T(8,128)(2,1)}, u32[]{:S(2)}) copy-start(bf16[864,64]{0,1:T(8,128)(2,1)} %param.18) | copy-start | bytes 331780
  198.1 8.4 %copy-start.8 = (bf16[1024,64]{0,1:T(8,128)(2,1)}, bf16[1024,64]{0,1:T(8,128)(2,1)S(1)}, u32[]{:S(2)}) copy-start(bf16[1024,64]{0,1:T(8,128)(2,1)S(1)} %convolution_convert_fusion.1) | copy-start | bytes 393220
  206.5 17.8 %copy-start.10 = (bf16[1024,64]{0,1:T(8,128)(2,1)}, bf16[1024,64]{0,1:T(8,128)(2,1)S(1)}, u32[]{:S(2)}) copy-start(bf16[1024,64]{0,1:T(8,128)(2,1)S(1)} %convolution_convert_fusion) | copy-start | bytes 393220
  206.5 0.7 copy-start.16
  242.3 1.2 copy-start.1
  265.8 150.8 %reduce-scatter.7.cloned.1.call-start = ((), (), s32[]{:S(2)}) async-start(), calls=%async_computation.7 | async-start | bytes 5898240
  295.9 0.9 copy-start.15
  295.9 1.3 copy-start.3
  296.8 51.9 %copy-start.9 = (bf16[1024,64]{0,1:T(8,128)(2,1)S(1)}, bf16[1024,64]{0,1:T(8,128)(2,1)}, u32[]{:S(2)}) copy-start(bf16[1024,64]{0,1:T(8,128)(2,1)} %copy-done.8) | copy-start | bytes 393220
  297.3 52.0 %copy-start.2 = (bf16[1024,864]{0,1:T(8,128)(2,1)S(1)}, bf16[1024,864]{0,1:T(8,128)(2,1)}, u32[]{:S(2)}) copy-start(bf16[1024,864]{0,1:T(8,128)(2,1)} %copy-done.1) | copy-start | bytes 5308420
  297.3 52.0 %copy-start.11 = (bf16[1024,64]{0,1:T(8,128)(2,1)S(1)}, bf16[1024,64]{0,1:T(8,128)(2,1)}, u32[]{:S(2)}) copy-start(bf16[1024,64]{0,1:T(8,128)(2,1)} %copy-done.10) | copy-start | bytes 393220
  297.3 2.0 collective-permute-start
  299.3 21.8 %collective-permute-start.1 = (f32[1024,128]{0,1:T(8,128)S(1)}, f32[1024,128]{0,1:T(8,128)S(1)}, u32[]{:S(2)}, u32[]{:S(2)}) collective-permute-start(f32[1024,128]{0,1:T(8,128)S(1)} %fusion.11), channel_id=1, source_target_pairs={{0,2},{1,3},{2,0},{3,1},{4,6},{5,7},{6,4},{7,5},{8,10},{9,11},{10,... | collective-permute-start | bytes 1572872 | tf_op jit(solution)/shard_map/ppermute | solution.py:45
  321.2 40.8 %copy-start.5 = (bf16[1024,320]{0,1:T(8,128)(2,1)S(1)}, bf16[1024,320]{0,1:T(8,128)(2,1)}, u32[]{:S(2)}) copy-start(bf16[1024,320]{0,1:T(8,128)(2,1)} %copy-done.4) | copy-start | bytes 1966084
  321.2 24.8 %collective-permute-start.2 = (f32[1024,128]{0,1:T(8,128)S(1)}, f32[1024,128]{0,1:T(8,128)S(1)}, u32[]{:S(2)}, u32[]{:S(2)}) collective-permute-start(f32[1024,128]{0,1:T(8,128)S(1)} %add.74), channel_id=1, source_target_pairs={{0,4},{1,5},{2,6},{3,7},{4,0},{5,1},{6,2},{7,3},{8,12},{9,13},{10,... | collective-permute-start | bytes 1572872 | tf_op jit(solution)/shard_map/ppermute | solution.py:45
  346.1 16.2 %copy-start.7 = (bf16[1024,320]{0,1:T(8,128)(2,1)S(1)}, bf16[1024,320]{0,1:T(8,128)(2,1)}, u32[]{:S(2)}) copy-start(bf16[1024,320]{0,1:T(8,128)(2,1)} %param.10) | copy-start | bytes 1966084
  346.1 15.8 %collective-permute-start.3 = (f32[1024,128]{0,1:T(8,128)S(1)}, f32[1024,128]{0,1:T(8,128)S(1)}, u32[]{:S(2)}, u32[]{:S(2)}) collective-permute-start(f32[1024,128]{0,1:T(8,128)S(1)} %add.75), channel_id=1, source_target_pairs={{0,8},{1,9},{2,10},{3,11},{4,12},{5,13},{6,14},{7,15},{8,0},{9,1},... | collective-permute-start | bytes 1572872 | tf_op jit(solution)/shard_map/ppermute | solution.py:45
  362.9 20.4 %collective-permute-start.4 = (f32[2368,64]{0,1:T(8,128)S(1)}, f32[2368,64]{0,1:T(8,128)S(1)}, u32[]{:S(2)}, u32[]{:S(2)}) collective-permute-start(f32[2368,64]{0,1:T(8,128)S(1)} %concatenate.7), channel_id=1, source_target_pairs={{0,16},{16,0},{32,48},{48,32},{64,80},{80,64},{96,112},{112,96},{1... | collective-permute-start | bytes 1818632 | tf_op jit(solution)/shard_map/ppermute | solution.py:45
  383.4 15.4 %collective-permute-start.5 = (f32[2368,64]{0,1:T(8,128)S(1)}, f32[2368,64]{0,1:T(8,128)S(1)}, u32[]{:S(2)}, u32[]{:S(2)}) collective-permute-start(f32[2368,64]{0,1:T(8,128)S(1)} %add.77), channel_id=1, source_target_pairs={{0,32},{16,48},{32,0},{48,16},{64,96},{80,112},{96,64},{112,80},{1... | collective-permute-start | bytes 1818632 | tf_op jit(solution)/shard_map/ppermute | solution.py:45
  398.9 16.1 %collective-permute-start.6 = (f32[2368,64]{0,1:T(8,128)S(1)}, f32[2368,64]{0,1:T(8,128)S(1)}, u32[]{:S(2)}, u32[]{:S(2)}) collective-permute-start(f32[2368,64]{0,1:T(8,128)S(1)} %add.78), channel_id=1, source_target_pairs={{0,64},{16,80},{32,96},{48,112},{64,0},{80,16},{96,32},{112,48},{1... | collective-permute-start | bytes 1818632 | tf_op jit(solution)/shard_map/ppermute | solution.py:45
Sparse Core Ops, SparseCore 0:
  79.0 24.5 all-gather.2
  145.1 24.6 all-gather.4
  265.9 21.9 reduce-scatter.4
  296.0 116.2 reduce-scatter.6
